TPU v7x, 128 devices: a whole 4x4x4 slice. The times are simulated.
128 devices in a mesh: row: 2 (over y_lo), col: 16 (over x, y_hi, core), mode: 4 (over z).
Axes of the slice: x: 4, y: 4 (y_hi: 2, y_lo: 2; y = y_hi * 2 + y_lo), z: 4, core: 2. Of those that a mesh axis runs over, the one named last changes fastest.
Arguments:
- object_slab: float32 [2, 4096, 4096], P(None, 'row', 'col'), may hold values from -4.2 to 4.2
- probe_modes: float32 [2, 4, 256, 256], P(None, 'mode'), may hold values from -4.2 to 4.2
- amplitudes: float32 [512, 256, 256], P(('row', 'col')), may hold values from 0.5 to 3.5
- scan_counts: int32 [32], replicated, may hold values from 1 to 16, as said below
- scan_positions: int32 [2, 512], P(None, ('row', 'col')), may hold values from 0 to 3840, as said below
Outputs:
- object_grad: float32 [2, 4096, 4096], P(None, 'row', 'col')
- probe_grad: float32 [2, 4, 256, 256], P(None, 'mode')
- position_grad: float32 [2, 512], P(None, ('row', 'col'))
Inputs may be any that keep to these rules, and one draw needn't show every extreme that they name: `scan_counts`: each tile holds between 1 and 16 patterns, and some tile holds exactly 16; a tile's active slots are its first ones. `scan_positions`: every slot's window starts inside the tile that owns the slot (slot p is owned by tile p // 16, tiles numbered row index * 16 + column index) and lies wholly inside the object; inactive slots also carry such positions.
All inputs are finite; a program needn't handle non-finite values.
Results may differ from a plain program's by a relative error of at most 0.0003.
Values sent between devices are 32-bit elements; how exact they have to be, the bound alone decides.
A program may use at most 128 MiB of HBM per device.

v0:
```python
import math
import functools
import numpy as np
import jax
import jax.numpy as jnp
from jax import lax
from jax.experimental import pallas as pl
from jax.experimental.pallas import tpu as pltpu
from jax.sharding import PartitionSpec as P

BF = jnp.bfloat16
F32 = jnp.float32
BATCH = 4
CH = 32


def hi_lo(x):
    hi = x.astype(BF)
    lo = (x - hi.astype(F32)).astype(BF)
    return hi, lo


def halves(table):
    table = table.astype(np.float32)
    hi = table.astype(BF)
    return hi, (table - hi.astype(np.float32)).astype(BF)


def angles(window, radix, q):
    part = window // radix
    n, j = np.arange(part)[:, None], np.arange(part)[None, :]
    angle = 2.0 * math.pi * ((n * (radix * j + q)) % window) / window
    return np.cos(angle) / math.sqrt(window), np.sin(angle) / math.sqrt(window)


def tables(window):
    right_f, right_i, left_f, left_i = [], [], [], []
    for q in range(2):
        c, s = angles(window, 2, q)
        for table, into in ((np.block([[c, -s], [s, c]]), right_f), (np.block([[c.T, s.T], [-s.T, c.T]]), right_i)):
            hi, lo = halves(table)
            into.append(np.concatenate([hi, lo, hi], axis=0))
    for q in range(4):
        c, s = angles(window, 4, q)
        for table, into in ((np.block([[c.T, s.T], [-s.T, c.T]]), left_f), (np.block([[c, -s], [s, c]]), left_i)):
            hi, lo = halves(table)
            top = np.concatenate([hi, hi], axis=1)
            into.append(np.concatenate([top, np.concatenate([lo, np.zeros_like(lo)], axis=1)], axis=0))
    order = np.concatenate([np.arange(0, window, 2), np.arange(1, window, 2)])
    shuffle = np.zeros((window, window), np.float32)
    shuffle[order, np.arange(window)] = 1.0
    return np.stack(right_f), np.stack(right_i), np.stack(left_f), np.stack(left_i), shuffle.astype(BF)


def cat(parts, axis):
    return jnp.concatenate(parts, axis=axis)


def mm(a, b):
    return jnp.dot(a, b, preferred_element_type=F32)


def make_compute(window, modes, slots, tile_rows, tile_cols, cols_n):
    w, half, quart = window, window // 2, window // 4
    ch = CH
    ext_rows, ext_cols = tile_rows + w, tile_cols + w

    def kernel(positions, counts, own, right, low, diag, probe, amps, rf, ri, lf, li, shuffle,
               g_own, g_right, g_low, g_diag, pg, along,
               ext, grad, amp_buf, win, fac, lhs, rhs, mid, far, near, amp_sem, sem):
        row_id, col_id, mine = place()
        count = counts[row_id * cols_n + col_id]
        def quarters(whole, parts):
            pairs = []
            for k in range(4):
                for t in range(2):
                    down = slice(tile_rows, ext_rows) if k >= 2 else slice(0, tile_rows)
                    pairs.append((whole.at[2 * (k % 2) + t, :, down, :], parts[k].at[:, :, 128 * t:128 * t + 128]))
            return pairs

        loads = [
            pltpu.make_async_copy(part, inside, sem.at[k])
            for k, (inside, part) in enumerate(quarters(ext, (own, right, low, diag)))
        ]
        for copy in loads:
            copy.start()

        def amp_copies(slot, place):
            return [
                pltpu.make_async_copy(
                    amps.at[slot, :, 128 * t:128 * t + 128], amp_buf.at[place, t], amp_sem.at[place, t]
                )
                for t in range(2)
            ]

        for copy in amp_copies(0, 0):
            copy.start()

        def clear(i, carry):
            at = pl.multiple_of(i * ch, ch)
            for c in range(2):
                for t in range(4):
                    grad[t, c, pl.ds(at, ch), :] = jnp.zeros((ch, 128), F32)
            return carry

        lax.fori_loop(0, ext_rows // ch, clear, 0)
        pg[...] = jnp.zeros(pg.shape, F32)

        def no_shift(i, carry):
            along[0, i] = 0.0
            along[1, i] = 0.0
            return carry

        lax.fori_loop(0, slots, no_shift, 0)
        for copy in loads:
            copy.wait()

        def put_lhs(parity, at, x):
            hi, lo = hi_lo(x)
            lhs[parity, at:at + ch, :w] = hi
            lhs[parity, at:at + ch, w:] = lo

        def put_rhs(m, q, at, x):
            hi, lo = hi_lo(x)
            rhs[m, q, at:at + ch, :] = hi
            rhs[m, q, half + at:half + at + ch, :] = lo

        def right_apply(m, table, into):
            rows = slice(m * w, (m + BATCH) * w)
            for parity in range(2):
                hi, lo = lhs[parity, rows, :w], lhs[parity, rows, w:]
                into[parity, rows, :] = mm(cat([hi, hi, lo], 1), table[parity])

        def left_apply(m, q, table):
            both = mm(table[q], rhs[m, q])
            return both[:half] + both[half:]

        def forward_rows(m):
            for r in range(0, quart, ch):
                y = [[], [], [], []]
                for parity in range(2):
                    x = [mid[parity, m * w + p * quart + r:m * w + p * quart + r + ch, :] for p in range(4)]
                    a, b, c, d = x[0] + x[2], x[1] + x[3], x[0] - x[2], x[1] - x[3]
                    y[0].append(a + b)
                    y[2].append(a - b)
                    turned = cat([d[:, half:], -d[:, :half]], 1)
                    y[1].append(c + turned)
                    y[3].append(c - turned)
                for q in range(4):
                    e, o = y[q]
                    put_rhs(m, q, r, cat([e[:, :half], o[:, :half]], 1))
                    put_rhs(m, q, quart + r, cat([e[:, half:], o[:, half:]], 1))
            for q in range(4):
                far[m, q] = left_apply(m, q, lf)

        def inverse_rows(m):
            for q in range(4):
                for r in range(0, quart, ch):
                    f = fac[q, r:r + ch, :]
                    for at in (r, quart + r):
                        put_rhs(m, q, at, f * far[m, q, at:at + ch, :])
            for q in range(4):
                far[m, q] = left_apply(m, q, li)
            for r in range(0, quart, ch):
                re = [far[m, q, r:r + ch, :] for q in range(4)]
                im = [far[m, q, quart + r:quart + r + ch, :] for q in range(4)]
                are, aim, bre, bim = re[0] + re[2], im[0] + im[2], re[1] + re[3], im[1] + im[3]
                cre, cim, dre, dim = re[0] - re[2], im[0] - im[2], re[1] - re[3], im[1] - im[3]
                outs = (
                    (are + bre, aim + bim), (cre - dim, cim + dre),
                    (are - bre, aim - bim), (cre + dim, cim - dre),
                )
                for p, (xre, xim) in enumerate(outs):
                    for parity in range(2):
                        cols = slice(parity * half, parity * half + half)
                        put_lhs(parity, m * w + p * quart + r, cat([xre[:, cols], xim[:, cols]], 1))

        def do_slot(slot, carry):
            row = positions[0, slot] - row_id * tile_rows
            col = positions[1, slot] - col_id * tile_cols
            tile_at = col // 128
            off = lax.rem(col, 128)
            back = lax.rem(w + 128 - off, w + 128)
            place_at = lax.rem(slot, 2)
            for copy in amp_copies(slot, place_at):
                copy.wait()

            @pl.when(slot + 1 < count)
            def _():
                for copy in amp_copies(slot + 1, 1 - place_at):
                    copy.start()

            for c in range(2):
                for r in range(0, w, ch):
                    wide = cat([ext[tile_at + t, c, pl.ds(row + r, ch), :] for t in range(3)], 1)
                    win[c, r:r + ch, :] = pltpu.roll(wide, back, 1)[:, :w]

            for q in range(4):
                a = cat([amp_buf[place_at, t, pl.ds(q, quart, stride=4), :] for t in range(2)], 1)
                a0, a1 = hi_lo(a)
                a2 = (a - a0.astype(F32) - a1.astype(F32)).astype(BF)
                stack = mm(cat([a0, a1, a2], 0), shuffle[...])
                fac[q] = stack[:quart] + stack[quart:2 * quart] + stack[2 * quart:]

            for m in range(modes):
                for r in range(0, w, ch):
                    vre, vim = win[0, r:r + ch, :], win[1, r:r + ch, :]
                    pre, pim = probe[0, m, r:r + ch, :], probe[1, m, r:r + ch, :]
                    are = pre * vre - pim * vim
                    aim = pre * vim + pim * vre
                    for parity in range(2):
                        if parity == 0:
                            x = cat([are[:, :half] + are[:, half:], aim[:, :half] + aim[:, half:]], 1)
                        else:
                            x = cat([are[:, :half] - are[:, half:], aim[:, :half] - aim[:, half:]], 1)
                        put_lhs(parity, m * w + r, x)
                if (m + 1) % BATCH == 0:
                    right_apply(m + 1 - BATCH, rf, mid)
                    for n in range(m + 1 - BATCH, m + 1):
                        forward_rows(n)

            for q in range(4):
                for r in range(0, quart, ch):
                    total = None
                    for m in range(modes):
                        re = far[m, q, r:r + ch, :]
                        im = far[m, q, quart + r:quart + r + ch, :]
                        term = re * re + im * im
                        total = term if total is None else total + term
                    fac[q, r:r + ch, :] = 0.25 * (1.0 - fac[q, r:r + ch, :] * lax.rsqrt(total + 0.5))

            for m in range(modes):
                inverse_rows(m)
                if (m + 1) % BATCH == 0:
                    right_apply(m + 1 - BATCH, ri, near)

            rows_sum = jnp.zeros((8, w), F32)
            cols_sum = jnp.zeros((8, w), F32)
            lanes = lax.broadcasted_iota(jnp.int32, (ch, w), 1)
            inner = (lanes >= 1) & (lanes <= w - 2)

            def near_of(m, r):
                at = m * w + r
                if not isinstance(m, int):
                    at = pl.multiple_of(at, ch)
                e, o = near[0, pl.ds(at, ch), :], near[1, pl.ds(at, ch), :]
                s, d = e + o, e - o
                return cat([s[:, :half], d[:, :half]], 1), cat([s[:, half:], d[:, half:]], 1)

            for r in range(0, w, ch):
                gre = gim = None
                for m in range(modes):
                    nre, nim = near_of(m, r)
                    pre, pim = probe[0, m, r:r + ch, :], probe[1, m, r:r + ch, :]
                    tre = pre * nre + pim * nim
                    tim = pre * nim - pim * nre
                    gre = tre if gre is None else gre + tre
                    gim = tim if gim is None else gim + tim
                for c, g in ((0, gre), (1, gim)):
                    spread = pltpu.roll(cat([g, jnp.zeros((ch, 128), F32)], 1), off, 1)
                    for t in range(3):
                        grad[tile_at + t, c, pl.ds(row + r, ch), :] += spread[:, 128 * t:128 * t + 128]
                vre, vim = win[0, r:r + ch, :], win[1, r:r + ch, :]
                nre, nim = near_of(mine, r)
                pg[0, r:r + ch, :] += vre * nre + vim * nim
                pg[1, r:r + ch, :] += vre * nim - vim * nre
                dre = pltpu.roll(vre, w - 1, 1) - pltpu.roll(vre, 1, 1)
                dim = pltpu.roll(vim, w - 1, 1) - pltpu.roll(vim, 1, 1)
                t = jnp.where(inner, gre * dre + gim * dim, 0.0)
                cols_sum = cols_sum + jnp.sum(t.reshape(ch // 8, 8, w), axis=0)
                lo_r, hi_r = max(r, 1), min(r + ch, w - 1)
                up = [ext_rows_slice(win, c, r + 1, ch, w) for c in range(2)]
                dn = [ext_rows_slice(win, c, r - 1, ch, w) for c in range(2)]
                t = gre * (up[0] - dn[0]) + gim * (up[1] - dn[1])
                if lo_r != r or hi_r != r + ch:
                    idx = lax.broadcasted_iota(jnp.int32, (ch, w), 0) + r
                    t = jnp.where((idx >= lo_r) & (idx < hi_r), t, 0.0)
                rows_sum = rows_sum + jnp.sum(t.reshape(ch // 8, 8, w), axis=0)
            along[0, slot] = jnp.sum(rows_sum) * (0.5 / w)
            along[1, slot] = jnp.sum(cols_sum) * (0.5 / w)
            return carry

        def ext_rows_slice(ref, c, start, size, width):
            if start < 0:
                return cat([ref[c, 0:1, :], ref[c, 0:size - 1, :]], 0)
            if start + size > w:
                return cat([ref[c, start:w, :], ref[c, w - 1:w, :]], 0)
            return ref[c, start:start + size, :]

        lax.fori_loop(0, count, do_slot, 0)
        stores = [
            pltpu.make_async_copy(inside, part, sem.at[k])
            for k, (inside, part) in enumerate(quarters(grad, (g_own, g_right, g_low, g_diag)))
        ]
        for copy in stores:
            copy.start()
        for copy in stores:
            copy.wait()

    hbm = pl.BlockSpec(memory_space=pl.ANY)
    vmem = pl.BlockSpec(memory_space=pltpu.VMEM)
    smem = pl.BlockSpec(memory_space=pltpu.SMEM)
    shape = jax.ShapeDtypeStruct
    return pl.pallas_call(
        kernel,
        name="slots",
        in_specs=[smem, smem, hbm, hbm, hbm, hbm, vmem, hbm, vmem, vmem, vmem, vmem, vmem],
        out_specs=[hbm, hbm, hbm, hbm, vmem, smem],
        out_shape=[
            shape((2, tile_rows, tile_cols), F32),
            shape((2, tile_rows, w), F32),
            shape((2, w, tile_cols), F32),
            shape((2, w, w), F32),
            shape((2, w, w), F32),
            shape((2, slots), F32),
        ],
        scratch_shapes=[
            pltpu.VMEM((ext_cols // 128, 2, ext_rows, 128), F32),
            pltpu.VMEM((ext_cols // 128, 2, ext_rows, 128), F32),
            pltpu.VMEM((2, 2, w, 128), F32),
            pltpu.VMEM((2, w, w), F32),
            pltpu.VMEM((4, quart, w), F32),
            pltpu.VMEM((2, modes * w, 2 * w), BF),
            pltpu.VMEM((modes, 4, w, w), BF),
            pltpu.VMEM((2, modes * w, w), F32),
            pltpu.VMEM((modes, 4, half, w), F32),
            pltpu.VMEM((2, modes * w, w), F32),
            pltpu.SemaphoreType.DMA((2, 2)),
            pltpu.SemaphoreType.DMA((8,)),
        ],
        compiler_params=pltpu.CompilerParams(vmem_limit_bytes=60 << 20),
        cost_estimate=pl.CostEstimate(flops=10**11, bytes_accessed=10**7, transcendentals=0),
    )


MESH = pl.DeviceIdType.MESH


def place():
    return lax.axis_index("row"), lax.axis_index("col"), lax.axis_index("mode")


def device(r, c, m):
    return {"row": r, "col": c, "mode": m}


def remote(src, dst, send, recv, to):
    return pltpu.make_async_remote_copy(
        src_ref=src, dst_ref=dst, send_sem=send, recv_sem=recv, device_id=to, device_id_type=MESH
    )


def greet(to):
    pl.semaphore_signal(pltpu.get_barrier_semaphore(), inc=1, device_id=to, device_id_type=MESH)


class Quarters:
    def __init__(self, src, dst, modes, rows, r, c, chunks, sems):
        me_r, me_c, m = place()
        self.m, self.modes, self.chunks = m, modes, chunks
        self.rows = rows // modes // chunks
        self.src, self.dst = src, dst
        self.ys, self.yr, self.zs, self.zr, self.ts, self.tr = sems
        self.peer = device(r, c, m)
        self.next = device(me_r, me_c, lax.rem(m + 1, modes))
        self.prev = device(me_r, me_c, lax.rem(m + modes - 1, modes))

    def part(self, ref, owner, i):
        at = pl.multiple_of((owner * self.chunks + i) * self.rows, self.rows)
        return ref.at[:, pl.ds(at, self.rows), :]

    def first(self, i):
        mine = self.part(self.src, self.m, i)
        return remote(mine, self.part(self.dst, self.m, i), self.ys.at[i], self.yr.at[i], self.peer)

    def ring(self, i, way):
        mine = self.part(self.dst, self.m, i)
        return remote(mine, mine, self.zs.at[way, i], self.zr.at[way, i], self.next if way == 0 else self.prev)

    def way(self, i):
        return 0 if i < self.chunks // 2 else 1

    def relay(self, i):
        back = self.modes - 1 if self.way(i) == 0 else 1
        block = self.part(self.dst, lax.rem(self.m + back, self.modes), i)
        return remote(block, block, self.ts.at[i], self.tr.at[i], self.next if self.way(i) == 0 else self.prev)

    def start(self):
        for i in range(self.chunks):
            self.first(i).start()

    def sent(self):
        for i in range(self.chunks):
            self.first(i).wait_send()

    def take(self, some=None):
        for i in range(self.chunks) if some is None else some:
            self.first(i).wait_recv()
            self.ring(i, 0).start()
            self.ring(i, 1).start()

    def turn(self):
        for i in range(self.chunks):
            self.ring(i, self.way(i)).wait_recv()
            self.relay(i).start()

    def finish(self):
        for i in range(self.chunks):
            self.ring(i, 1 - self.way(i)).wait_recv()
            self.relay(i).wait_recv()
        for i in range(self.chunks):
            self.ring(i, 0).wait_send()
            self.ring(i, 1).wait_send()
            self.relay(i).wait_send()


STRIP, EDGE = 4, 2


def quarter_sems(chunks):
    one = pltpu.SemaphoreType.DMA((chunks,))
    two = pltpu.SemaphoreType.DMA((2, chunks))
    return [one, one, two, two, one, one]


def when(cond, *steps):
    @pl.when(cond)
    def _():
        for step in steps:
            step()


def make_spread(window, modes, tile_rows, tile_cols, rows_n, cols_n):
    w = window

    def kernel(tile, probe, right, low, diag, gathered, *sems):
        quarter, (one_s, one_r, p_s, p_r, x_s, x_r, own_sem) = sems[:6], sems[6:]
        r, c, m = place()
        core = lax.rem(c, 2)
        other = c + 1 - 2 * core
        odd, even = core == 1, core == 0
        has_left, has_right = c > 0, c < cols_n - 1
        top = tile.at[:, pl.ds(0, w), :]

        for k in range(1, modes):
            greet(device(r, c, lax.rem(m + k, modes)))
        greet(device(r, other, m))
        greet(device(rows_n - 1 - r, c, m))
        count = modes + 1
        away = jnp.where(odd, jnp.minimum(c + 1, cols_n - 1), jnp.maximum(c - 1, 0))
        has_away = jnp.where(odd, has_right, has_left)

        @pl.when(has_away)
        def _():
            greet(device(r, away, m))

        has_diag = has_away & jnp.where(odd, r == 0, r == 1)

        @pl.when(has_diag)
        def _():
            greet(device(rows_n - 1 - r, away, m))

        pl.semaphore_wait(
            pltpu.get_barrier_semaphore(),
            count + has_away.astype(jnp.int32) + has_diag.astype(jnp.int32),
        )

        strip = Quarters(tile, right, modes, tile_rows, r, away, STRIP, quarter)
        whole = remote(tile, right, one_s.at[0], one_r.at[0], device(r, other, m))
        down = remote(top, low, one_s.at[1], one_r.at[1], device(rows_n - 1 - r, c, m))
        corner = remote(top, diag, one_s.at[2], one_r.at[2], device(rows_n - 1 - r, away, m))
        corner_on = remote(low, diag, one_s.at[2], one_r.at[2], device(r, other, m))

        def probe_copy(k):
            half = gathered.at[pl.ds(core, 1), pl.ds(m, 1)]
            return remote(
                probe.at[pl.ds(core, 1)], half, p_s.at[k], p_r.at[k], device(r, c, lax.rem(m + k, modes))
            )

        def probe_pass(k):
            half = gathered.at[pl.ds(core, 1), pl.ds(lax.rem(m + modes - k, modes), 1)]
            return remote(half, half, x_s.at[k], x_r.at[k], device(r, other, m))

        @pl.when(even & has_left)
        def _():
            strip.start()

        @pl.when(r == 1)
        def _():
            down.start()

        @pl.when(even & has_diag)
        def _():
            corner.start()

        for k in (1, 3, 2):
            probe_copy(k).start()

        @pl.when(odd)
        def _():
            whole.start()

        keep = pltpu.make_async_copy(probe, gathered.at[:, pl.ds(m, 1)], own_sem)
        keep.start()

        @pl.when(odd & has_right)
        def _():
            strip.take()

        @pl.when(r == 0)
        def _():
            down.wait_recv()

        @pl.when(odd & (r == 0))
        def _():
            corner_on.start()

        for k in (1, 3, 2):
            probe_copy(k).wait_recv()
            probe_pass(k).start()

        @pl.when(odd & has_right)
        def _():
            strip.turn()
            strip.finish()

        @pl.when(odd & has_diag)
        def _():
            corner.wait_recv()

        @pl.when(even)
        def _():
            whole.wait_recv()

        @pl.when(even & (r == 0))
        def _():
            corner_on.wait_recv()

        for k in (1, 3, 2):
            probe_pass(k).wait_recv()
            probe_pass(k).wait_send()
            probe_copy(k).wait_send()
        keep.wait()

        @pl.when(odd)
        def _():
            whole.wait_send()

        @pl.when(odd & (r == 0))
        def _():
            corner_on.wait_send()

        @pl.when(even & has_left)
        def _():
            strip.sent()

        @pl.when(r == 1)
        def _():
            down.wait_send()

        @pl.when(even & has_diag)
        def _():
            corner.wait_send()

    hbm = pl.BlockSpec(memory_space=pl.ANY)
    shape = jax.ShapeDtypeStruct
    return pl.pallas_call(
        kernel,
        name="spread",
        in_specs=[hbm, hbm],
        out_specs=[hbm] * 4,
        out_shape=[
            shape((2, tile_rows, tile_cols), F32),
            shape((2, w, tile_cols), F32),
            shape((2, w, tile_cols), F32),
            shape((2, modes, w, w), F32),
        ],
        scratch_shapes=quarter_sems(STRIP) + [pltpu.SemaphoreType.DMA((3,))] * 2
        + [pltpu.SemaphoreType.DMA((modes,))] * 4 + [pltpu.SemaphoreType.DMA],
        compiler_params=pltpu.CompilerParams(collective_id=0, has_side_effects=True),
    )


def make_collect(window, modes, tile_rows, tile_cols, rows_n, cols_n):
    w = window
    chips = rows_n * cols_n // 2
    piece = 2 * w // chips

    def kernel(g_right, g_low, g_diag, pg, right, low, diag, total, *sems):
        strip_sems, low_sems, diag_sems = sems[:6], sems[6:12], sems[12:18]
        one_s, one_r, x_s, x_r, y_s, y_r, a_s, a_r, b_s, b_r, in_sem, pair, got, mine = sems[18:]
        r, c, m = place()
        core = lax.rem(c, 2)
        chip = r * (cols_n // 2) + c // 2
        other = c + 1 - 2 * core
        odd, even = core == 1, core == 0
        away = jnp.where(odd, jnp.minimum(c + 1, cols_n - 1), jnp.maximum(c - 1, 0))
        has_away = jnp.where(odd, c < cols_n - 1, c > 0)
        flip = rows_n - 1 - r
        over = jnp.where(r == 0, jnp.minimum(c + 1, cols_n - 1), jnp.maximum(c - 1, 0))
        has_over = jnp.where(r == 0, c < cols_n - 1, c > 0)

        def partner(k):
            p = lax.rem(chip + k, chips)
            return device(p // (cols_n // 2), 2 * lax.rem(p, cols_n // 2) + core, m)

        def hello(k, carry):
            greet(partner(k))
            return carry

        greet(device(r, other, m))
        for k in (1, modes - 1):
            greet(device(r, c, lax.rem(m + k, modes)))
        when(has_away, lambda: greet(device(r, away, m)))
        when(has_over, lambda: greet(device(flip, over, m)))
        when(even, lambda: greet(device(flip, c, m)))
        when(odd, lambda: lax.fori_loop(1, chips, hello, 0))
        pl.semaphore_wait(
            pltpu.get_barrier_semaphore(),
            3 + jnp.where(odd, chips - 1, 1) + has_away.astype(jnp.int32) + has_over.astype(jnp.int32),
        )

        strip = Quarters(g_right, right, modes, tile_rows, r, away, STRIP, strip_sems)
        down = Quarters(g_low, low, modes, w, flip, c, EDGE, low_sems)
        corner = Quarters(g_diag, diag, modes, w, flip, over, EDGE, diag_sems)
        whole = remote(g_right, right, one_s, one_r, device(r, other, m))
        swap = remote(pg, pair.at[0], x_s, x_r, device(r, other, m))
        own = pltpu.make_async_copy(pg, pair.at[1], in_sem)
        at_chip = pl.ds(pl.multiple_of(chip * piece, piece), piece)
        rest = got.at[pl.ds(1, chips - 1)]
        many = total.at[pl.ds(0, (chips - 1) * piece), :]
        keep = pltpu.make_async_copy(mine, total.at[at_chip, :], in_sem)
        give = remote(total, total, y_s, y_r, device(r, other, m))

        def scatter_go(k, carry):
            p = lax.rem(chip + k, chips)
            rows = pl.ds(pl.multiple_of(p * piece, piece), piece)
            remote(pair.at[1, rows, :], got.at[k], a_s, a_r, partner(k)).start()
            return carry

        def share_go(k, carry):
            remote(mine, total.at[at_chip, :], b_s, b_r, partner(k)).start()
            return carry

        def add(k, acc):
            return acc + got[k]

        def sum_pair():
            own.wait()
            swap.wait_recv()
            pair[1] = pair[0] + pair[1]
            lax.fori_loop(1, chips, scatter_go, 0)

        def sum_plane():
            pltpu.make_async_copy(rest, rest, a_r).wait()
            mine[...] = lax.fori_loop(1, chips, add, pair[1, at_chip, :]) * (1.0 / 16.0)
            keep.start()
            lax.fori_loop(1, chips, share_go, 0)

        def sum_give():
            keep.wait()
            pltpu.make_async_copy(many, many, b_r).wait()
            give.start()

        def sum_end():
            pltpu.make_async_copy(rest, rest, a_s).wait()
            pltpu.make_async_copy(many, many, b_s).wait()
            give.wait_send()

        when(even, swap.start)
        when(odd, own.start)
        when(odd & has_away, strip.start)
        when(r == 0, down.start)
        when((r == 0) & has_over, corner.start)
        when(even, whole.start)
        when(odd, sum_pair)
        when(even & has_away, strip.take)
        when(r == 1, down.take)
        when((r == 1) & has_over, corner.take)
        when(odd, sum_plane)
        when(even & has_away, strip.turn)
        when(r == 1, down.turn)
        when((r == 1) & has_over, corner.turn)
        when(odd, sum_give)
        when(even & has_away, strip.finish)
        when(r == 1, down.finish)
        when((r == 1) & has_over, corner.finish)
        when(odd, whole.wait_recv)
        when(even, give.wait_recv)
        when(even, swap.wait_send)
        when(odd, sum_end)
        when(odd & has_away, strip.sent)
        when(r == 0, down.sent)
        when((r == 0) & has_over, corner.sent)
        when(even, whole.wait_send)

    hbm = pl.BlockSpec(memory_space=pl.ANY)
    shape = jax.ShapeDtypeStruct
    dma = pltpu.SemaphoreType.DMA
    return pl.pallas_call(
        kernel,
        name="collect",
        in_specs=[hbm] * 4,
        out_specs=[hbm] * 4,
        out_shape=[
            shape((2, tile_rows, tile_cols), F32),
            shape((2, w, tile_cols), F32),
            shape((2, w, tile_cols), F32),
            shape((2 * w, w), F32),
        ],
        scratch_shapes=quarter_sems(STRIP) + quarter_sems(EDGE) + quarter_sems(EDGE) + [dma] * 11
        + [pltpu.VMEM((2, 2 * w, w), F32), pltpu.VMEM((chips, piece, w), F32), pltpu.VMEM((piece, w), F32)],
        compiler_params=pltpu.CompilerParams(collective_id=1, has_side_effects=True),
    )


def make_finish(window, tile_rows, tile_cols):
    w = window
    blocks = tile_rows // w

    def kernel(own, strip, low, diag, total, grad, probe, a, b, e, s_a, s_b, s_e, s_out):
        r, c, m = place()
        below, inner = r > 0, c > 0

        def rows(k):
            return pl.ds(k * w, w)

        loads = [
            [
                pltpu.make_async_copy(own.at[:, rows(k), :], a.at[:, rows(k), :], s_a.at[k]),
                pltpu.make_async_copy(strip.at[:, rows(k), :], b.at[:, rows(k), :], s_b.at[k]),
            ]
            for k in range(blocks)
        ]
        edges = [pltpu.make_async_copy(src, e.at[n], s_e.at[n]) for n, src in enumerate((low, diag, total))]
        for k in reversed(range(blocks)):
            for copy in loads[k]:
                copy.start()
        for copy in edges:
            copy.start()
        stores = [pltpu.make_async_copy(a.at[:, rows(k), :], grad.at[:, rows(k), :], s_out.at[k]) for k in range(blocks)]

        def add(k, x):
            for part in range(2):
                a[part, k * w:k * w + w, :] += x[part]

        for k in reversed(range(blocks)):
            for copy in loads[k]:
                copy.wait()
            when(inner, lambda: add(k, b.at[:, rows(k), :]))
            if k == 0:
                for copy in edges:
                    copy.wait()
                when(below, lambda: add(0, e.at[0]))
                when(below & inner, lambda: add(0, e.at[1]))
                last = pltpu.make_async_copy(e.at[2], probe, s_out.at[blocks])
                last.start()
            stores[k].start()
        for copy in stores + [last]:
            copy.wait()

    hbm = pl.BlockSpec(memory_space=pl.ANY)
    dma = pltpu.SemaphoreType.DMA
    tile = (2, tile_rows, tile_cols)
    return pl.pallas_call(
        kernel,
        name="finish",
        in_specs=[hbm] * 5,
        out_specs=[hbm] * 2,
        out_shape=[jax.ShapeDtypeStruct(tile, F32), jax.ShapeDtypeStruct((2, w, w), F32)],
        scratch_shapes=[
            pltpu.VMEM(tile, F32), pltpu.VMEM(tile, F32), pltpu.VMEM((3, 2, w, w), F32),
            dma((blocks,)), dma((blocks,)), dma((3,)), dma((blocks + 1,)),
        ],
        compiler_params=pltpu.CompilerParams(vmem_limit_bytes=60 << 20),
    )


def per_device(object_slab, probe_modes, amplitudes, scan_counts, scan_positions):
    window = probe_modes.shape[-1]
    tile_rows, tile_cols = object_slab.shape[1:]
    slots = amplitudes.shape[0]
    modes, cols_n, rows_n = (lax.axis_size(a) for a in ("mode", "col", "row"))
    sizes = (window, modes, tile_rows, tile_cols, rows_n, cols_n)
    right, low, diag, probe = make_spread(*sizes)(object_slab, probe_modes)
    consts = [jnp.asarray(t) for t in tables(window)]
    compute = make_compute(window, modes, slots, tile_rows, tile_cols, cols_n)
    g_own, g_right, g_low, g_diag, pg, shift = compute(
        scan_positions, scan_counts, object_slab, right, low, diag, probe, amplitudes, *consts
    )
    from_left, from_up, from_diag, total = make_collect(*sizes)(
        g_right, g_low, g_diag, pg.reshape(2 * window, window)
    )
    grad, probe_grad = make_finish(window, tile_rows, tile_cols)(
        g_own, from_left, from_up, from_diag, total.reshape(2, window, window)
    )
    return (grad, probe_grad.reshape(2, 1, window, window), shift)


def solution(mesh):
    in_specs = (
        P(None, "row", "col"),
        P(None, "mode", None, None),
        P(("row", "col"), None, None),
        P(),
        P(None, ("row", "col")),
    )
    out_specs = (P(None, "row", "col"), P(None, "mode", None, None), P(None, ("row", "col")))
    return jax.shard_map(
        per_device, mesh=mesh, in_specs=in_specs, out_specs=out_specs, check_vma=False
    )
```

profile of v0, /device:TPU:10, one launch (start us, length us, event | category | flops | bytes accessed | tf_op | source)
XLA Modules:
  0.0 163.8 jit_solution(3762513266917355364)
XLA Ops:
  0.6 27.4 %spread.1 = (f32[2,2048,256]{2,1,0:T(8,128)}, f32[2,256,256]{2,1,0:T(8,128)}, f32[2,256,256]{2,1,0:T(8,128)}, f32[2,4,256,256]{3,2,1,0:T(8,128)}) custom-call(f32[2,2048,256]{2,1,0:T(8,128)} %own.1, f32[2,1,256,256]{3,2,1,0:T(8,128)} %probe.1), custom_call_target="tpu_custom_call" | custom-call | tf_op jit(solution)/shard_map/spread/pallas_call | solution.py:785
  28.0 50.4 %slots.1 = (f32[2,2048,256]{2,1,0:T(8,128)}, f32[2,2048,256]{2,1,0:T(8,128)}, f32[2,256,256]{2,1,0:T(8,128)}, f32[2,256,256]{2,1,0:T(8,128)}, f32[2,256,256]{2,1,0:T(8,128)}, /*index=5*/f32[2,16]{1,0:T(2,128)}) custom-call(s32[2,16]{1,0:T(2,128)} %positions.1, s32[32]{0:T(128)} %counts.1, f32[2,2048,256]{2,1,0:T(8,128)} %own.1, ...), custom_call_target="tpu_custom_call" | custom-call | flops 99999997952 | bytes 10000000 | tf_op jit(solution)/shard_map/slots/pallas_call | solution.py:788
  78.4 79.1 %collect.1 = (f32[2,2048,256]{2,1,0:T(8,128)}, f32[2,256,256]{2,1,0:T(8,128)}, f32[2,256,256]{2,1,0:T(8,128)}, f32[512,256]{1,0:T(8,128)}) custom-call(f32[2,2048,256]{2,1,0:T(8,128)} %get-tuple-element.24.g_right, f32[2,256,256]{2,1,0:T(8,128)} %get-tuple-element.25.g_low, f32[2,256,256]{2,1,0:T(8,128)} %get-tuple-element.26.g_diag, f32[512,256]{1,0:T(8,128)} %bitcast.6), custom_call_target="tpu_custom_call" | custom-call | tf_op jit(solution)/shard_map/collect/pallas_call | solution.py:791
  157.5 6.3 %finish.1 = (f32[2,2048,256]{2,1,0:T(8,128)}, f32[2,256,256]{2,1,0:T(8,128)}) custom-call(f32[2,2048,256]{2,1,0:T(8,128)} %get-tuple-element.23.own, f32[2,2048,256]{2,1,0:T(8,128)} %get-tuple-element.28.strip, f32[2,256,256]{2,1,0:T(8,128)} %get-tuple-element.29.low, f32[2,256,256]{2,1,0:T(8,128)} %get-tuple-element.30.diag, f32[2,256,256]{2,1,0:T(8,128)} %bitcast.5), custom_call_target="tpu_custom_call" | custom-call | tf_op jit(solution)/shard_map/finish/pallas_call | solution.py:794
where the time goes:
time: 164 us
  Pallas kernels  163 us (99%)
    pallas_call x1, Pallas kernels, per_device(): make_collect(*sizes)(g_right, g_low, g_diag, pg.reshape(2 * window, window))  79.1 us
    pallas_call x1, Pallas kernels, per_device(): compute(scan_positions, scan_counts, object_slab, right, low, diag, probe...  50.4 us
    pallas_call x1, Pallas kernels, per_device(): right, low, diag, probe = make_spread(*sizes)(object_slab, probe_modes)  27.4 us
    pallas_call x1, Pallas kernels, per_device(): make_finish(window, tile_rows, tile_cols)  6.29 us

commit v1 on v0

--- a/solution.py
+++ b/solution.py
@@ -587,8 +587,8 @@
     piece = 2 * w // chips
 
     def kernel(g_right, g_low, g_diag, pg, right, low, diag, total, *sems):
-        strip_sems, low_sems, diag_sems = sems[:6], sems[6:12], sems[12:18]
-        one_s, one_r, x_s, x_r, y_s, y_r, a_s, a_r, b_s, b_r, in_sem, pair, got, mine = sems[18:]
+        strip_sems = sems[:6]
+        one_s, one_r, d_s, d_r, e_s, e_r, x_s, x_r, y_s, y_r, a_s, a_r, b_s, b_r, in_sem, pair, got, mine = sems[6:]
         r, c, m = place()
         core = lax.rem(c, 2)
         chip = r * (cols_n // 2) + c // 2
@@ -621,8 +621,8 @@
         )
 
         strip = Quarters(g_right, right, modes, tile_rows, r, away, STRIP, strip_sems)
-        down = Quarters(g_low, low, modes, w, flip, c, EDGE, low_sems)
-        corner = Quarters(g_diag, diag, modes, w, flip, over, EDGE, diag_sems)
+        down = remote(g_low, low, d_s, d_r, device(flip, c, m))
+        corner = remote(g_diag, diag, e_s, e_r, device(flip, over, m))
         whole = remote(g_right, right, one_s, one_r, device(r, other, m))
         swap = remote(pg, pair.at[0], x_s, x_r, device(r, other, m))
         own = pltpu.make_async_copy(pg, pair.at[1], in_sem)
@@ -675,23 +675,19 @@
         when(even, whole.start)
         when(odd, sum_pair)
         when(even & has_away, strip.take)
-        when(r == 1, down.take)
-        when((r == 1) & has_over, corner.take)
         when(odd, sum_plane)
         when(even & has_away, strip.turn)
-        when(r == 1, down.turn)
-        when((r == 1) & has_over, corner.turn)
         when(odd, sum_give)
         when(even & has_away, strip.finish)
-        when(r == 1, down.finish)
-        when((r == 1) & has_over, corner.finish)
+        when(r == 1, down.wait_recv)
+        when((r == 1) & has_over, corner.wait_recv)
         when(odd, whole.wait_recv)
         when(even, give.wait_recv)
         when(even, swap.wait_send)
         when(odd, sum_end)
         when(odd & has_away, strip.sent)
-        when(r == 0, down.sent)
-        when((r == 0) & has_over, corner.sent)
+        when(r == 0, down.wait_send)
+        when((r == 0) & has_over, corner.wait_send)
         when(even, whole.wait_send)
 
     hbm = pl.BlockSpec(memory_space=pl.ANY)
@@ -708,7 +704,7 @@
             shape((2, w, tile_cols), F32),
             shape((2 * w, w), F32),
         ],
-        scratch_shapes=quarter_sems(STRIP) + quarter_sems(EDGE) + quarter_sems(EDGE) + [dma] * 11
+        scratch_shapes=quarter_sems(STRIP) + [dma] * 15
         + [pltpu.VMEM((2, 2 * w, w), F32), pltpu.VMEM((chips, piece, w), F32), pltpu.VMEM((piece, w), F32)],
         compiler_params=pltpu.CompilerParams(collective_id=1, has_side_effects=True),
     )

time: 164 us -> 170 us (1.037)
  the two profiles are of different devices: /device:TPU:10 before, /device:TPU:1 now
where the time goes in v1:
time: 170 us; the launch traced here: 169 us
  Pallas kernels  168 us (99%)
    pallas_call x1, Pallas kernels, per_device(): compute(scan_positions, scan_counts, object_slab, right, low, diag, probe...  63.6 us
    pallas_call x1, Pallas kernels, per_device(): make_collect(*sizes)(g_right, g_low, g_diag, pg.reshape(2 * window, window))  59.7 us
    pallas_call x1, Pallas kernels, per_device(): right, low, diag, probe = make_spread(*sizes)(object_slab, probe_modes)  38.5 us
    pallas_call x1, Pallas kernels, per_device(): make_finish(window, tile_rows, tile_cols)  6.18 us

profile of v1, /device:TPU:1, one launch (start us, length us, event | category | flops | bytes accessed | tf_op | source)
XLA Modules:
  0.0 168.7 jit_solution(4057773165361005206)
XLA Ops:
  0.6 38.5 %spread.1 = (f32[2,2048,256]{2,1,0:T(8,128)}, f32[2,256,256]{2,1,0:T(8,128)}, f32[2,256,256]{2,1,0:T(8,128)}, f32[2,4,256,256]{3,2,1,0:T(8,128)}) custom-call(f32[2,2048,256]{2,1,0:T(8,128)} %own.1, f32[2,1,256,256]{3,2,1,0:T(8,128)} %probe.1), custom_call_target="tpu_custom_call" | custom-call | tf_op jit(solution)/shard_map/spread/pallas_call | solution.py:781
  39.2 63.6 %slots.1 = (f32[2,2048,256]{2,1,0:T(8,128)}, f32[2,2048,256]{2,1,0:T(8,128)}, f32[2,256,256]{2,1,0:T(8,128)}, f32[2,256,256]{2,1,0:T(8,128)}, f32[2,256,256]{2,1,0:T(8,128)}, /*index=5*/f32[2,16]{1,0:T(2,128)}) custom-call(s32[2,16]{1,0:T(2,128)} %positions.1, s32[32]{0:T(128)} %counts.1, f32[2,2048,256]{2,1,0:T(8,128)} %own.1, ...), custom_call_target="tpu_custom_call" | custom-call | flops 99999997952 | bytes 10000000 | tf_op jit(solution)/shard_map/slots/pallas_call | solution.py:784
  102.8 59.7 %collect.1 = (f32[2,2048,256]{2,1,0:T(8,128)}, f32[2,256,256]{2,1,0:T(8,128)}, f32[2,256,256]{2,1,0:T(8,128)}, f32[512,256]{1,0:T(8,128)}) custom-call(f32[2,2048,256]{2,1,0:T(8,128)} %get-tuple-element.24.g_right, f32[2,256,256]{2,1,0:T(8,128)} %get-tuple-element.25.g_low, f32[2,256,256]{2,1,0:T(8,128)} %get-tuple-element.26.g_diag, f32[512,256]{1,0:T(8,128)} %bitcast.6), custom_call_target="tpu_custom_call" | custom-call | tf_op jit(solution)/shard_map/collect/pallas_call | solution.py:787
  162.5 6.2 %finish.1 = (f32[2,2048,256]{2,1,0:T(8,128)}, f32[2,256,256]{2,1,0:T(8,128)}) custom-call(f32[2,2048,256]{2,1,0:T(8,128)} %get-tuple-element.23.own, f32[2,2048,256]{2,1,0:T(8,128)} %get-tuple-element.28.strip, f32[2,256,256]{2,1,0:T(8,128)} %get-tuple-element.29.low, f32[2,256,256]{2,1,0:T(8,128)} %get-tuple-element.30.diag, f32[2,256,256]{2,1,0:T(8,128)} %bitcast.5), custom_call_target="tpu_custom_call" | custom-call | tf_op jit(solution)/shard_map/finish/pallas_call | solution.py:790
